TPU v7x, 512 devices: a whole 4x4x16 slice. The times are simulated.
512 devices in a mesh: tm: 128 (over z, y, core), chan: 4 (over x).
Axes of the slice: x: 4, y: 4, z: 16, core: 2. Of those that a mesh axis runs over, the one named last changes fastest.
Arguments:
- markov: float32 [16384, 256, 4], P('tm', 'chan'), may hold values from -6 to 6
- sketch: float32 [16384, 4, 64], P('tm'), may hold values from -0.0234375 to 0.0234375
Outputs:
- basis: float32 [16384, 256, 64], P('tm', 'chan')
- factor: float32 [64, 64], replicated
All inputs are finite; a program needn't handle non-finite values.
Results may differ from a plain program's by a relative error of at most 0.000098.
Values sent between devices are 32-bit elements; how exact they have to be, the bound alone decides.
A program may use at most 128 MiB of HBM per device.

v0:
```python
import math

import jax
import jax.numpy as jnp
from jax import lax
from jax.sharding import PartitionSpec as P

HIGHEST_PREC = lax.Precision.HIGHEST


def circle(first, second, modulus):
    angle = (first[:, None] * second[None, :] % modulus).astype(jnp.float32) * (
        2.0 * math.pi / modulus
    )
    return (jnp.cos(angle), jnp.sin(angle))


def matmul_rows(matrix, blocks):
    return jnp.einsum("ab,bgw->agw", matrix, blocks, precision=HIGHEST_PREC)


def plain_dot(left, right):
    return jnp.dot(left, right, precision=HIGHEST_PREC)


def gram_of(matrix):
    return jnp.einsum("nr,ns->rs", matrix, matrix, precision=HIGHEST_PREC)


def product(left, right):
    return jnp.einsum("kpm,kmr->kpr", left, right, precision=HIGHEST_PREC)


def total_factor(gram_part, row_total):
    summed = lax.psum(gram_part, ("tm", "chan"))
    result = jnp.linalg.cholesky(summed / row_total)
    return result


def body(markov, sketch):
    seq_len = markov.shape[0]
    shards = lax.axis_size("tm")
    per_group = seq_len // shards
    whole_len = seq_len * shards
    own_index = lax.axis_index("tm")
    channels = markov.shape[1]
    inputs = markov.shape[2]
    columns = sketch.shape[2]
    row_total = whole_len * channels * lax.axis_size("chan")
    small_index = jnp.arange(shards, dtype=jnp.int32)
    time_index = jnp.arange(seq_len, dtype=jnp.int32)
    freq_index = own_index + shards * time_index
    cos_small, sin_small = circle(small_index, small_index, shards)
    cos_large, sin_large = circle(freq_index, time_index, whole_len)
    markov_blocks = markov.reshape(shards, per_group, channels * inputs)
    sketch_blocks = sketch.reshape(shards, per_group, inputs * columns)
    pieces = (
        lax.all_to_all(markov_blocks, "tm", split_axis=0, concat_axis=0, tiled=True),
        lax.all_to_all(sketch_blocks, "tm", split_axis=0, concat_axis=0, tiled=True),
    )
    results = []
    for piece_block in pieces:
        results.append(matmul_rows(cos_small, piece_block))
        results.append(-matmul_rows(sin_small, piece_block))
    spread = tuple(results)
    pieces = (
        lax.all_to_all(spread[0], "tm", split_axis=0, concat_axis=1, tiled=True),
        lax.all_to_all(spread[1], "tm", split_axis=0, concat_axis=1, tiled=True),
        lax.all_to_all(spread[2], "tm", split_axis=0, concat_axis=1, tiled=True),
        lax.all_to_all(spread[3], "tm", split_axis=0, concat_axis=1, tiled=True),
    )
    results = []
    for place in range(0, len(pieces), 2):
        real_part = pieces[place].reshape(seq_len, -1)
        imag_part = pieces[place + 1].reshape(seq_len, -1)
        results.append(plain_dot(cos_large, real_part) + plain_dot(sin_large, imag_part))
        results.append(plain_dot(cos_large, imag_part) - plain_dot(sin_large, real_part))
    markov_re, markov_im, sketch_re, sketch_im = tuple(results)
    markov_re = markov_re.reshape(seq_len, channels, inputs)
    markov_im = markov_im.reshape(seq_len, channels, inputs)
    sketch_re = sketch_re.reshape(seq_len, inputs, columns)
    sketch_im = sketch_im.reshape(seq_len, inputs, columns)
    spec_re = (product(markov_re, sketch_re) + product(markov_im, sketch_im)).reshape(
        seq_len * channels, columns
    )
    spec_im = (product(markov_im, sketch_re) - product(markov_re, sketch_im)).reshape(
        seq_len * channels, columns
    )
    identity_m = jnp.eye(columns, dtype=jnp.float32)
    real_part = spec_re.reshape(seq_len, channels * columns)
    imag_part = spec_im.reshape(seq_len, channels * columns)
    width = real_part.shape[1]
    turned_re = plain_dot(cos_large.T, real_part) - plain_dot(sin_large.T, imag_part)
    turned_im = plain_dot(sin_large.T, real_part) + plain_dot(cos_large.T, imag_part)
    pieces = (
        lax.all_to_all(
            turned_re.reshape(shards, per_group, width),
            "tm",
            split_axis=0,
            concat_axis=0,
            tiled=True,
        ),
        lax.all_to_all(
            turned_im.reshape(shards, per_group, width),
            "tm",
            split_axis=0,
            concat_axis=0,
            tiled=True,
        ),
    )
    mixed = (matmul_rows(cos_small, pieces[0]) - matmul_rows(sin_small, pieces[1])) / whole_len
    returned = lax.all_to_all(mixed, "tm", split_axis=0, concat_axis=1, tiled=True)
    result_time = returned.reshape(seq_len, width)
    signal = result_time
    signal = signal.reshape(seq_len * channels, columns)
    gram_part = gram_of(signal)
    lower_factor = total_factor(gram_part, row_total)
    inverse_t = jax.scipy.linalg.solve_triangular(lower_factor, identity_m, lower=True).T
    result = plain_dot(signal, inverse_t)
    return (result.reshape(seq_len, channels, columns), lower_factor.T)


def solution(mesh):
    return jax.shard_map(
        body,
        mesh=mesh,
        in_specs=(P("tm", "chan", None), P("tm", None, None)),
        out_specs=(P("tm", "chan", None), P()),
        check_vma=False,
    )
```

profile of v0, /device:TPU:1, one launch (start us, length us, event | category | flops | bytes accessed | tf_op | source)
XLA Modules:
  0.0 682.6 jit_solution(10656477915658200802)
XLA Ops:
  2.3 20.6 %all-to-all-start = ((f32[128,1,256]{2,1,0:T(1,128)}), f32[128,1,256]{2,1,0:T(1,128)S(1)}, u32[]{:S(2)}, u32[]{:S(2)}) async-start(f32[128,1,256]{2,1,0:T(1,128)} %copy.57), calls=%async_computation | async-start | bytes 262144 | tf_op jit(solution)/shard_map/all_to_all | solution.py:58
  24.5 14.3 %all-to-all-done = f32[128,1,256]{2,1,0:T(1,128)S(1)} async-done(((f32[128,1,256]{2,1,0:T(1,128)}), f32[128,1,256]{2,1,0:T(1,128)S(1)}, u32[]{:S(2)}, u32[]{:S(2)}) %all-to-all-start) | async-done | bytes 131104 | tf_op jit(solution)/shard_map/all_to_all | solution.py:58
  38.8 7.2 %all-to-all-start.3 = ((f32[128,1,256]{2,1,0:T(1,128)}), f32[128,1,256]{2,1,0:T(1,128)S(1)}, u32[]{:S(2)}, u32[]{:S(2)}) async-start(f32[128,1,256]{2,1,0:T(1,128)} %copy.61), calls=%async_computation.3 | async-start | bytes 262144 | tf_op jit(solution)/shard_map/all_to_all | solution.py:59
  47.4 14.6 %all-to-all-done.3 = f32[128,1,256]{2,1,0:T(1,128)S(1)} async-done(((f32[128,1,256]{2,1,0:T(1,128)}), f32[128,1,256]{2,1,0:T(1,128)S(1)}, u32[]{:S(2)}, u32[]{:S(2)}) %all-to-all-start.3) | async-done | bytes 131104 | tf_op jit(solution)/shard_map/all_to_all | solution.py:59
  62.0 7.3 %all-to-all-start.2 = ((f32[128,1,256]{2,1,0:T(1,128)}), f32[128,1,256]{2,1,0:T(1,128)S(1)}, u32[]{:S(2)}, u32[]{:S(2)}) async-start(f32[128,1,256]{2,1,0:T(1,128)} %copy.59), calls=%async_computation.2 | async-start | bytes 262144 | tf_op jit(solution)/shard_map/all_to_all | solution.py:68
  70.6 14.7 %all-to-all-done.2 = f32[128,1,256]{2,1,0:T(1,128)S(1)} async-done(((f32[128,1,256]{2,1,0:T(1,128)}), f32[128,1,256]{2,1,0:T(1,128)S(1)}, u32[]{:S(2)}, u32[]{:S(2)}) %all-to-all-start.2) | async-done | bytes 131104 | tf_op jit(solution)/shard_map/all_to_all | solution.py:68
  85.2 7.2 %all-to-all-start.1 = ((f32[128,1,256]{2,1,0:T(1,128)}), f32[128,1,256]{2,1,0:T(1,128)S(1)}, u32[]{:S(2)}, u32[]{:S(2)}) async-start(f32[128,1,256]{2,1,0:T(1,128)} %copy.58), calls=%async_computation.1 | async-start | bytes 262144 | tf_op jit(solution)/shard_map/all_to_all | solution.py:67
  93.8 14.7 %all-to-all-done.1 = f32[128,1,256]{2,1,0:T(1,128)S(1)} async-done(((f32[128,1,256]{2,1,0:T(1,128)}), f32[128,1,256]{2,1,0:T(1,128)S(1)}, u32[]{:S(2)}, u32[]{:S(2)}) %all-to-all-start.1) | async-done | bytes 131104 | tf_op jit(solution)/shard_map/all_to_all | solution.py:67
  108.5 7.7 %all-to-all-start.5 = ((f32[128,1,256]{2,1,0:T(1,128)}), f32[128,1,256]{2,1,0:T(1,128)S(1)}, u32[]{:S(2)}, u32[]{:S(2)}) async-start(f32[128,1,256]{2,1,0:T(1,128)} %copy.63), calls=%async_computation.5 | async-start | bytes 262144 | tf_op jit(solution)/shard_map/all_to_all | solution.py:70
  118.6 13.5 %all-to-all-done.5 = f32[128,1,256]{2,1,0:T(1,128)S(1)} async-done(((f32[128,1,256]{2,1,0:T(1,128)}), f32[128,1,256]{2,1,0:T(1,128)S(1)}, u32[]{:S(2)}, u32[]{:S(2)}) %all-to-all-start.5) | async-done | bytes 131104 | tf_op jit(solution)/shard_map/all_to_all | solution.py:70
  132.1 7.2 %all-to-all-start.4 = ((f32[128,1,256]{2,1,0:T(1,128)}), f32[128,1,256]{2,1,0:T(1,128)S(1)}, u32[]{:S(2)}, u32[]{:S(2)}) async-start(f32[128,1,256]{2,1,0:T(1,128)} %copy.62), calls=%async_computation.4 | async-start | bytes 262144 | tf_op jit(solution)/shard_map/all_to_all | solution.py:69
  141.4 13.8 %all-to-all-done.4 = f32[128,1,256]{2,1,0:T(1,128)S(1)} async-done(((f32[128,1,256]{2,1,0:T(1,128)}), f32[128,1,256]{2,1,0:T(1,128)S(1)}, u32[]{:S(2)}, u32[]{:S(2)}) %all-to-all-start.4) | async-done | bytes 131104 | tf_op jit(solution)/shard_map/all_to_all | solution.py:69
  157.4 6.7 fusion.151
  164.1 8.4 %fusion.150 = f32[128,64,64]{2,1,0:T(8,128)} fusion(f32[128,64,4]{1,2,0:T(4,128)S(1)} %copy.65, f32[128,4,64]{2,1,0:T(4,128)S(1)} %copy.66), kind=kOutput, calls=%fused_computation.161 | convolution fusion | flops 25165824 | bytes 2359296 | tf_op jit(solution)/shard_map/kpm,kmr->kpr/dot_general | solution.py:31
  172.5 8.3 %convolution_subtract_fusion.2 = f32[128,64,64]{2,1,0:T(8,128)} fusion(f32[128,64,64]{2,1,0:T(8,128)S(1)} %fusion.151, f32[128,64,4]{1,2,0:T(4,128)S(1)} %copy.65, f32[128,4,64]{2,1,0:T(4,128)S(1)} %copy.70), kind=kOutput, calls=%fused_computation.7 | convolution fusion | flops 25690112 | bytes 4456448 | tf_op jit(solution)/shard_map/kpm,kmr->kpr/dot_general | solution.py:31
  184.6 9.8 %convolution_add_fusion.1 = f32[128,64,64]{2,1,0:T(8,128)} fusion(f32[128,64,64]{2,1,0:T(8,128)} %fusion.150, f32[128,64,4]{1,2,0:T(4,128)S(1)} %copy.69, f32[128,4,64]{2,1,0:T(4,128)S(1)} %copy.70), kind=kOutput, calls=%fused_computation.8 | convolution fusion | flops 25690112 | bytes 4456448 | tf_op jit(solution)/shard_map/kpm,kmr->kpr/dot_general | solution.py:31
  209.0 8.3 %all-to-all-start.6 = ((f32[128,1,4096]{2,1,0:T(1,128)}), f32[128,1,4096]{2,1,0:T(1,128)}, u32[]{:S(2)}, u32[]{:S(2)}) async-start(f32[128,1,4096]{2,1,0:T(1,128)} %copy.77), calls=%async_computation.6 | async-start | bytes 4194304 | tf_op jit(solution)/shard_map/all_to_all | solution.py:96
  226.8 85.7 %all-to-all-done.6 = f32[128,1,4096]{2,1,0:T(1,128)} async-done(((f32[128,1,4096]{2,1,0:T(1,128)}), f32[128,1,4096]{2,1,0:T(1,128)}, u32[]{:S(2)}, u32[]{:S(2)}) %all-to-all-start.6) | async-done | bytes 2097184 | tf_op jit(solution)/shard_map/all_to_all | solution.py:96
  312.6 11.3 %all-to-all-start.7 = ((f32[128,1,4096]{2,1,0:T(1,128)}), f32[128,1,4096]{2,1,0:T(1,128)S(1)}, u32[]{:S(2)}, u32[]{:S(2)}) async-start(f32[128,1,4096]{2,1,0:T(1,128)} %copy.78), calls=%async_computation.7 | async-start | bytes 4194304 | tf_op jit(solution)/shard_map/all_to_all | solution.py:103
  329.9 89.8 %all-to-all-done.7 = f32[128,1,4096]{2,1,0:T(1,128)S(1)} async-done(((f32[128,1,4096]{2,1,0:T(1,128)}), f32[128,1,4096]{2,1,0:T(1,128)S(1)}, u32[]{:S(2)}, u32[]{:S(2)}) %all-to-all-start.7) | async-done | bytes 2097184 | tf_op jit(solution)/shard_map/all_to_all | solution.py:103
  426.7 107.0 %all_to_all.65 = f32[128,1,4096]{2,1,0:T(1,128)S(1)} all-to-all(f32[128,1,4096]{2,1,0:T(1,128)S(1)} %copy.79), channel_id=1, replica_groups=mesh['tm'=128,'chan'=4] {'tm'}, dimensions={0} | all-to-all | bytes 4194304 | tf_op jit(solution)/shard_map/all_to_all | solution.py:112
  533.7 7.3 %reduce.6 = f32[128,4096]{1,0:T(8,128)} reduce(f32[128,1,4096]{2,1,0:T(1,128)S(1)} %all_to_all.65, f32[]{:T(128)} %constant.86), dimensions={1}, to_apply=%all_to_all.26.reduce_sub_computation | reduce | bytes 4194308 | tf_op jit(solution)/shard_map/all_to_all | solution.py:112
  545.8 10.4 %fusion.152 = f32[64,64]{0,1:T(8,128)S(1)} fusion(f32[8192,64]{1,0:T(8,128)} %reshape_reshape.11), kind=kOutput, calls=%fused_computation.163 | convolution fusion | flops 402653184 | bytes 2113536 | tf_op jit(solution)/shard_map/nr,ns->rs/dot_general | solution.py:27
  556.2 104.1 %psum.7 = f32[64,64]{0,1:T(8,128)S(1)} all-reduce(f32[64,64]{0,1:T(8,128)S(1)} %fusion.152), channel_id=1, replica_groups=mesh['tm'=128,'chan'=4] {'tm','chan'}, use_global_device_ids=true, to_apply=%region_0.1 | all-reduce | flops 4096 | bytes 32768 | tf_op jit(solution)/shard_map/psum | solution.py:35
  (51 shorter events, 81.5 us)
Async XLA Ops:
  2.3 36.6 %all-to-all-start = ((f32[128,1,256]{2,1,0:T(1,128)}), f32[128,1,256]{2,1,0:T(1,128)S(1)}, u32[]{:S(2)}, u32[]{:S(2)}) async-start(f32[128,1,256]{2,1,0:T(1,128)} %copy.57), calls=%async_computation | async-start | bytes 262144 | tf_op jit(solution)/shard_map/all_to_all | solution.py:58
  38.8 23.2 %all-to-all-start.3 = ((f32[128,1,256]{2,1,0:T(1,128)}), f32[128,1,256]{2,1,0:T(1,128)S(1)}, u32[]{:S(2)}, u32[]{:S(2)}) async-start(f32[128,1,256]{2,1,0:T(1,128)} %copy.61), calls=%async_computation.3 | async-start | bytes 262144 | tf_op jit(solution)/shard_map/all_to_all | solution.py:59
  62.0 23.3 %all-to-all-start.2 = ((f32[128,1,256]{2,1,0:T(1,128)}), f32[128,1,256]{2,1,0:T(1,128)S(1)}, u32[]{:S(2)}, u32[]{:S(2)}) async-start(f32[128,1,256]{2,1,0:T(1,128)} %copy.59), calls=%async_computation.2 | async-start | bytes 262144 | tf_op jit(solution)/shard_map/all_to_all | solution.py:68
  85.2 23.2 %all-to-all-start.1 = ((f32[128,1,256]{2,1,0:T(1,128)}), f32[128,1,256]{2,1,0:T(1,128)S(1)}, u32[]{:S(2)}, u32[]{:S(2)}) async-start(f32[128,1,256]{2,1,0:T(1,128)} %copy.58), calls=%async_computation.1 | async-start | bytes 262144 | tf_op jit(solution)/shard_map/all_to_all | solution.py:67
  108.5 23.6 %all-to-all-start.5 = ((f32[128,1,256]{2,1,0:T(1,128)}), f32[128,1,256]{2,1,0:T(1,128)S(1)}, u32[]{:S(2)}, u32[]{:S(2)}) async-start(f32[128,1,256]{2,1,0:T(1,128)} %copy.63), calls=%async_computation.5 | async-start | bytes 262144 | tf_op jit(solution)/shard_map/all_to_all | solution.py:70
  132.1 23.1 %all-to-all-start.4 = ((f32[128,1,256]{2,1,0:T(1,128)}), f32[128,1,256]{2,1,0:T(1,128)S(1)}, u32[]{:S(2)}, u32[]{:S(2)}) async-start(f32[128,1,256]{2,1,0:T(1,128)} %copy.62), calls=%async_computation.4 | async-start | bytes 262144 | tf_op jit(solution)/shard_map/all_to_all | solution.py:69
  209.0 103.6 %all-to-all-start.6 = ((f32[128,1,4096]{2,1,0:T(1,128)}), f32[128,1,4096]{2,1,0:T(1,128)}, u32[]{:S(2)}, u32[]{:S(2)}) async-start(f32[128,1,4096]{2,1,0:T(1,128)} %copy.77), calls=%async_computation.6 | async-start | bytes 4194304 | tf_op jit(solution)/shard_map/all_to_all | solution.py:96
  312.6 107.1 %all-to-all-start.7 = ((f32[128,1,4096]{2,1,0:T(1,128)}), f32[128,1,4096]{2,1,0:T(1,128)S(1)}, u32[]{:S(2)}, u32[]{:S(2)}) async-start(f32[128,1,4096]{2,1,0:T(1,128)} %copy.78), calls=%async_computation.7 | async-start | bytes 4194304 | tf_op jit(solution)/shard_map/all_to_all | solution.py:103
where the time goes:
time: 692 us; the launch traced here: 683 us
  waiting for transfers between devices  261 us (38%)
  blocking collectives  211 us (30%)
  matrix products  78.4 us (11%)
  starting transfers between devices  76.6 us (11%)
  local copies, waits for them, and re-layouts  34.7 us (5%)
  other arithmetic  19.3 us (3%)
    all_to_all x1, blocking collectives, body(): lax.all_to_all(mixed, 'tm', split_axis=0, concat_axis=1, tiled=True)  107 us
    psum x1, blocking collectives, total_factor(): summed = lax.psum(gram_part, ('tm', 'chan'))  104 us
    all_to_all x1, waiting for transfers between devices, body(): lax.all_to_all(turned_im.reshape(shards, per_group, width), 'tm', split_a...  89.8 us
    all_to_all x1, waiting for transfers between devices, body(): lax.all_to_all(turned_re.reshape(shards, per_group, width), 'tm', split_a...  85.7 us
    dot_general x4, matrix products, product(): return jnp.einsum('kpm,kmr->kpr', left, right, precision=HIGHEST_PREC)  33.2 us
    dot_general x13, matrix products, plain_dot(): return jnp.dot(left, right, precision=HIGHEST_PREC)  21.6 us
    all_to_all x1, starting transfers between devices, body(): lax.all_to_all(markov_blocks, 'tm', split_axis=0, concat_axis=0, tiled=True)  20.6 us
    all_to_all x1, waiting for transfers between devices, body(): lax.all_to_all(spread[1], 'tm', split_axis=0, concat_axis=1, tiled=True)  14.7 us
  transfers between devices with their start and end apart: 8, of which 8 were waited for; matrix products, arithmetic and copies ran while one was open for 4% of the time, Pallas kernels for 0%

commit v1 on v0

v1 whole, which is shorter than its diff:
```python
import functools

import jax
import jax.numpy as jnp
import ml_dtypes
import numpy as np
from jax import lax
from jax.experimental import pallas as pl
from jax.experimental.pallas import tpu as pltpu
from jax.sharding import PartitionSpec as P

HIGH = lax.Precision.HIGH
HIGHEST = lax.Precision.HIGHEST
MESH = pl.DeviceIdType.MESH
GROUP = 8


def reduce_kernel(depth, width, gram_ref, out_ref, first, mine, along, total, own, got,
                  send1, recv1, send2, recv2, send3, recv3):
    tm = lax.axis_index("tm")
    ch = lax.axis_index("chan")
    plane = tm // GROUP
    seat = tm - plane * GROUP

    def at(zi, si, ci):
        return (zi * GROUP + si, ci)

    barrier = pltpu.get_barrier_semaphore()
    for k in range(1, GROUP):
        pl.semaphore_signal(barrier, inc=1, device_id=at(plane, lax.rem(seat + k, GROUP), ch), device_id_type=MESH)
    for k in range(1, depth):
        pl.semaphore_signal(barrier, inc=1, device_id=at(lax.rem(plane + k, depth), seat, ch), device_id_type=MESH)
    for c in range(1, width):
        for k in range(GROUP):
            pl.semaphore_signal(barrier, inc=1, device_id=at(plane, lax.rem(seat + k, GROUP), lax.rem(ch + c, width)), device_id_type=MESH)
    pl.semaphore_wait(barrier, GROUP - 1 + depth - 1 + (width - 1) * GROUP)

    copies = []
    for k in range(1, GROUP):
        to = lax.rem(seat + k, GROUP)
        copies.append(pltpu.make_async_remote_copy(
            src_ref=gram_ref.at[to], dst_ref=first.at[k - 1],
            send_sem=send1.at[k - 1], recv_sem=recv1.at[k - 1],
            device_id=at(plane, to, ch), device_id_type=MESH))
    for copy in copies:
        copy.start()
    value = gram_ref[seat]
    for copy in copies:
        copy.wait()
    for k in range(1, GROUP):
        value = value + first[k - 1]
    mine[...] = value
    copies = []
    for k in range(1, depth):
        copies.append(pltpu.make_async_remote_copy(
            src_ref=mine, dst_ref=along.at[k - 1],
            send_sem=send2.at[k - 1], recv_sem=recv2.at[k - 1],
            device_id=at(lax.rem(plane + k, depth), seat, ch), device_id_type=MESH))
    for copy in copies:
        copy.start()
    for copy in copies:
        copy.wait()
    total[...] = jnp.zeros_like(total)
    for z in range(depth):
        back = lax.rem(plane - z + depth, depth)

        @pl.when(back == 0)
        def _():
            total[...] += mine[...]

        @pl.when(back != 0)
        def _():
            total[...] += along[lax.max(back - 1, 0)]
    own[...] = total[...]
    copies = []
    for c in range(width):
        for k in range(GROUP):
            if c == 0 and k == 0:
                continue
            slot = c * GROUP + k
            copies.append(pltpu.make_async_remote_copy(
                src_ref=own, dst_ref=got.at[slot],
                send_sem=send3.at[slot], recv_sem=recv3.at[slot],
                device_id=at(plane, lax.rem(seat + k, GROUP), lax.rem(ch + c, width)), device_id_type=MESH))
    for copy in copies:
        copy.start()
    got[0] = own[...]
    for copy in copies:
        copy.wait()
    for s in range(GROUP):
        k = lax.rem(seat - s + GROUP, GROUP)
        acc = jnp.zeros_like(own)
        for c in range(width):
            acc = acc + got[lax.rem(ch - c + width, width) * GROUP + k]
        out_ref[s] = acc


def total_gram(part, depth, width):
    tile = (8, 64)
    return pl.pallas_call(
        functools.partial(reduce_kernel, depth, width),
        out_shape=jax.ShapeDtypeStruct((GROUP,) + tile, jnp.float32),
        in_specs=[pl.BlockSpec(memory_space=pltpu.VMEM)],
        out_specs=pl.BlockSpec(memory_space=pltpu.VMEM),
        scratch_shapes=[
            pltpu.VMEM((GROUP - 1,) + tile, jnp.float32),
            pltpu.VMEM(tile, jnp.float32),
            pltpu.VMEM((depth - 1,) + tile, jnp.float32),
            pltpu.VMEM(tile, jnp.float32),
            pltpu.VMEM(tile, jnp.float32),
            pltpu.VMEM((width * GROUP,) + tile, jnp.float32),
            pltpu.SemaphoreType.DMA((GROUP - 1,)),
            pltpu.SemaphoreType.DMA((GROUP - 1,)),
            pltpu.SemaphoreType.DMA((depth - 1,)),
            pltpu.SemaphoreType.DMA((depth - 1,)),
            pltpu.SemaphoreType.DMA((width * GROUP,)),
            pltpu.SemaphoreType.DMA((width * GROUP,)),
        ],
        compiler_params=pltpu.CompilerParams(collective_id=1, has_side_effects=True),
    )(part.reshape((GROUP,) + tile)).reshape(64, 64)


def split(x):
    high = x.astype(jnp.bfloat16)
    return high, (x - high.astype(jnp.float32)).astype(jnp.bfloat16)


def outer(a, b):
    return lax.dot_general(a, b, (((1,), (1,)), ((), ())), preferred_element_type=jnp.float32)


def inner(a, b):
    return jnp.dot(a, b, preferred_element_type=jnp.float32)


def waves(block):
    n = np.arange(block)
    f = np.arange(block)
    angle = (2.0 * np.pi / (4 * block)) * ((n[None, :] * (2 * f[:, None] + 1)) % (4 * block))
    forward = np.stack([np.cos(angle), -np.sin(angle)], axis=1).reshape(2 * block, block)
    backward = np.concatenate([np.cos(angle).T, -np.sin(angle).T], axis=1) / block

    def pieces(x):
        high = x.astype(ml_dtypes.bfloat16)
        return high, (x - high.astype(np.float64)).astype(ml_dtypes.bfloat16)

    fh, fl = pieces(forward)
    bh, bl = pieces(backward)
    return (jnp.asarray(np.concatenate([fh, fh], axis=1)), jnp.asarray(fl),
            jnp.asarray(bh), jnp.asarray(bl))


def spectrum_kernel(block, shards, rows, x_ref, s_ref, fhh_ref, fl_ref, bh_ref, bl_ref,
                    sig_ref, gram_ref, hx, hs, mix):
    step = pl.program_id(0)
    last = pl.num_programs(0) - 1
    me = lax.axis_index("tm")

    def transform(slab, dst):
        src = slab.reshape(shards * rows, block)

        @pl.loop(0, rows // 2)
        def _(pair):
            p = pair * 2
            x = jnp.concatenate([
                src[pl.ds(p, shards, stride=rows), :],
                src[pl.ds(p + 1, shards, stride=rows), :]], axis=0)
            high, low = split(x)
            both = jnp.concatenate([high, low], axis=1)
            out = outer(fhh_ref[...], both) + outer(fl_ref[...], high)
            dst[pl.ds(p, 2 * block, stride=rows), :] = out[:, :shards]
            dst[pl.ds(p + 1, 2 * block, stride=rows), :] = out[:, shards:]

    transform(x_ref, hx)
    transform(s_ref, hs)

    def product(f):
        at = pl.multiple_of(f * 2 * rows, 2 * rows)
        h = hx[pl.ds(at, 2 * rows), :]
        t_re = hs[pl.ds(at, rows), :]
        t_im = hs[pl.ds(at + rows, rows), :]
        sign = (1 - 2 * lax.rem(f, 2)).astype(jnp.float32)
        here = pltpu.roll(jnp.concatenate([t_re, t_im], axis=0), me, 1)
        past = pltpu.roll(jnp.concatenate([-t_im, t_re], axis=0), me + 1, 1)
        t = here + sign * past
        hh, hl = split(h)
        th, tl = split(t)
        return outer(jnp.concatenate([hh, hl], axis=1), jnp.concatenate([th, th], axis=1)) + outer(hh, tl)

    @pl.when(step == 0)
    def _():
        @pl.loop(0, block)
        def _(f):
            mix[pl.ds(f, 2 * rows, stride=block), :] = product(f)

    @pl.when(step != 0)
    def _():
        @pl.loop(0, block)
        def _(f):
            mix[pl.ds(f, 2 * rows, stride=block), :] += product(f)

    @pl.when(step == last)
    def _():
        gram_ref[...] = jnp.zeros_like(gram_ref)

        @pl.loop(0, rows // 2)
        def _(pair):
            def parts(p):
                zero = mix[pl.ds(pl.multiple_of(p * block, block), block), :]
                one = mix[pl.ds(pl.multiple_of((rows + p) * block, block), block), :]
                return zero + pltpu.roll(one, rows, 1), one - pltpu.roll(zero, rows, 1)

            re0, im0 = parts(pair * 2)
            re1, im1 = parts(pair * 2 + 1)
            lane = lax.broadcasted_iota(jnp.int32, re0.shape, 1)
            re = jnp.where(lane < rows, re0, pltpu.roll(re1, rows, 1))
            im = jnp.where(lane < rows, im0, pltpu.roll(im1, rows, 1))
            high, low = split(jnp.concatenate([re, im], axis=0))
            out = inner(bh_ref[...], high) + inner(bh_ref[...], low) + inner(bl_ref[...], high)
            sig = out.T
            sig_ref[pl.ds(pl.multiple_of(pair * 2 * rows, 2 * rows), 2 * rows), :] = sig
            gram_ref[...] += lax.dot_general(
                sig, sig, (((1,), (1,)), ((), ())), precision=HIGHEST,
                preferred_element_type=jnp.float32)


def image(all_m, all_s, block, shards, rows, inputs):
    tables = waves(block)
    assert block == shards == 2 * rows
    whole = lambda x: pl.BlockSpec(x.shape, lambda m: (0, 0), pipeline_mode=pl.Buffered(1))
    slab = pl.BlockSpec((shards, None, rows, block), lambda m: (0, m, 0, 0))
    return pl.pallas_call(
        functools.partial(spectrum_kernel, block, shards, rows),
        grid=(inputs,),
        out_shape=(jax.ShapeDtypeStruct((rows * rows, block), jnp.float32),
                   jax.ShapeDtypeStruct((2 * rows, 2 * rows), jnp.float32)),
        in_specs=[slab, slab] + [whole(x) for x in tables],
        out_specs=(pl.BlockSpec((rows * rows, block), lambda m: (0, 0)),
                   pl.BlockSpec((2 * rows, 2 * rows), lambda m: (0, 0))),
        scratch_shapes=[pltpu.VMEM((2 * block * rows, shards), jnp.float32),
                        pltpu.VMEM((2 * block * rows, shards), jnp.float32),
                        pltpu.VMEM((2 * rows * block, 2 * rows), jnp.float32)],
        compiler_params=pltpu.CompilerParams(
            dimension_semantics=("arbitrary",), vmem_limit_bytes=60 * 2**20),
    )(all_m, all_s, *tables)


def body(markov, sketch):
    block, channels, inputs = markov.shape
    columns = sketch.shape[2]
    shards = lax.axis_size("tm")
    width = lax.axis_size("chan")
    row_total = block * shards * channels * width

    own_m = markov.transpose(2, 1, 0)
    own_s = sketch.transpose(1, 2, 0)
    all_m = lax.all_gather(own_m, "tm", axis=0, tiled=False)
    all_s = lax.all_gather(own_s, "tm", axis=0, tiled=False)
    sig, gram_two = image(all_m, all_s, block, shards, channels, inputs)
    signal = sig.reshape(channels, columns, block)
    gram_part = gram_two[:columns, :columns] + gram_two[columns:, columns:]
    gram = total_gram(gram_part, shards // GROUP, width)
    lower = jnp.linalg.cholesky(gram / row_total)
    eye = jnp.eye(columns, dtype=jnp.float32)
    inverse_t = jax.scipy.linalg.solve_triangular(lower, eye, lower=True).T
    basis = jnp.einsum("prb,rs->bps", signal, inverse_t, precision=HIGH)
    return basis, lower.T


def solution(mesh):
    return jax.shard_map(
        body,
        mesh=mesh,
        in_specs=(P("tm", "chan", None), P("tm", None, None)),
        out_specs=(P("tm", "chan", None), P()),
        check_vma=False,
    )
```

time: 692 us -> 681 us (0.984); the launches traced: 683 us -> 681 us
  Pallas kernels: 0 us -> 324 us
  blocking collectives: 211 us -> 0 us
  starting transfers between devices: 76.6 us -> 0.08 us
  matrix products: 78.4 us -> 4.1 us
  waiting for transfers between devices: 261 us -> 321 us
  local copies, waits for them, and re-layouts: 34.7 us -> 2.34 us
  between operations: 1.41 us -> 14.1 us
    pallas_call x0 -> x2, Pallas kernels: none -> 324 us  [the longest x1 298 us: image(): pl.pallas_call(functools.partial(spectrum_kernel, block, shards, rows), g...]
    all_gather x0 -> x2, waiting for transfers between devices: none -> 321 us  [the longest x1 165 us: body(): all_s = lax.all_gather(own_s, 'tm', axis=0, tiled=False)]
    all_to_all x8 -> x0, waiting for transfers between devices: 261 us -> none  [the longest x1 89.8 us: body(): lax.all_to_all(turned_im.reshape(shards, per_group, width), 'tm', split_a...]
    all_to_all x1 -> x0, blocking collectives: 107 us -> none  [body(): lax.all_to_all(mixed, 'tm', split_axis=0, concat_axis=1, tiled=True)]
    psum x1 -> x0, blocking collectives: 104 us -> none  [total_factor(): summed = lax.psum(gram_part, ('tm', 'chan'))]
    all_to_all x8 -> x0, starting transfers between devices: 76.6 us -> none  [the longest x1 20.6 us: body(): lax.all_to_all(markov_blocks, 'tm', split_axis=0, concat_axis=0, tiled=True)]
    dot_general x24 -> x1, matrix products: 78.1 us -> 3.87 us  [body(): basis = jnp.einsum('prb,rs->bps', signal, inverse_t, precision=HIGH)]
    reshape x8 -> x0, local copies, waits for them, and re-layouts: 10.9 us -> none  [the longest x1 3.48 us: body(): turned_im.reshape(shards, per_group, width)]
  transfers between devices with their start and end apart: 8 -> 2, of which waited for: 8 -> 2; matrix products, arithmetic and copies ran while one was open for 4% -> 0% of each run, Pallas kernels for 0% -> 0%
where the time goes in v1:
time: 681 us
  Pallas kernels  324 us (48%)
  waiting for transfers between devices  321 us (47%)
  other arithmetic  15.1 us (2%)
  between operations  14.1 us (2%)
    pallas_call x1, Pallas kernels, image(): pl.pallas_call(functools.partial(spectrum_kernel, block, shards, rows), g...  298 us
    all_gather x1, waiting for transfers between devices, body(): all_s = lax.all_gather(own_s, 'tm', axis=0, tiled=False)  165 us
    all_gather x1, waiting for transfers between devices, body(): all_m = lax.all_gather(own_m, 'tm', axis=0, tiled=False)  156 us
    pallas_call x1, Pallas kernels, total_gram(): pl.pallas_call(functools.partial(reduce_kernel, depth, width), out_shape=...  26.1 us
  transfers between devices with their start and end apart: 2, of which 2 were waited for; matrix products, arithmetic and copies ran while one was open for 0% of the time, Pallas kernels for 0%

profile of v1, /device:TPU:1, one launch (start us, length us, event | category | flops | bytes accessed | tf_op | source)
XLA Modules:
  0.0 680.7 jit_solution(5962096498835005027)
XLA Ops:
  7.2 0.0 all-gather.7.cloned.1.call-start
  7.2 0.7 all-gather.7.cloned.1.call-update
  7.9 0.0 all-gather.5.cloned.1.call-start
  7.9 1.6 copy.19
  9.5 0.0 all-gather.5.cloned.1.call-update
  9.5 164.5 %all-gather.7.cloned.1.call-done = f32[512,64,128]{2,1,0:T(8,128)} async-done(((f32[4,64,128]{2,1,0:T(8,128)}), f32[512,64,128]{2,1,0:T(8,128)}) %all-gather.7.cloned.1.call-update) | async-done | bytes 16777232 | tf_op jit(solution)/shard_map/all_gather | solution.py:258
  174.1 156.1 %all-gather.5.cloned.1.call-done = f32[512,64,128]{2,1,0:T(8,128)} async-done(((f32[4,64,128]{2,1,0:T(8,128)}), f32[512,64,128]{2,1,0:T(8,128)}) %all-gather.5.cloned.1.call-update) | async-done | bytes 16777232 | tf_op jit(solution)/shard_map/all_gather | solution.py:257
  330.2 297.5 %shard_map.77 = (f32[4096,128]{1,0:T(8,128)}, f32[128,128]{1,0:T(8,128)}) custom-call(f32[128,4,64,128]{3,2,1,0:T(8,128)} %bitcast.31, f32[128,4,64,128]{3,2,1,0:T(8,128)} %bitcast.30, bf16[256,256]{1,0:T(8,128)(2,1)} %constant.54.clone.fhh_ref, bf16[256,128]{1,0:T(8,128)(2,1)} %constant.55.clone.fl_ref, bf16[128,256]{1,0:T(8,128)(2,1)} %constant.56.clone.bh_ref, ...), custom_call_target="tpu_custom_call" | custom-call | tf_op jit(solution)/shard_map/pallas_call | solution.py:232
  627.7 1.5 add_bitcast_fusion.gram_ref
  629.2 26.1 %shard_map.78 = f32[8,8,64]{2,1,0:T(8,128)} custom-call(f32[8,8,64]{2,1,0:T(8,128)} %add_bitcast_fusion.gram_ref), custom_call_target="tpu_custom_call" | custom-call | tf_op jit(solution)/shard_map/pallas_call | solution.py:100
  655.3 0.8 multiply_bitcast_fusion
  656.1 0.1 copy.16
  656.2 0.8 fusion.1
  656.9 5.8 cholesky.17
  662.8 0.6 compare_reduce_fusion
  663.5 0.7 fusion.2
  664.1 0.7 copy.17
  664.8 4.9 custom-call.7
  669.7 0.2 convolution_bitcast_fusion.1
  669.9 3.9 convolution_bitcast_fusion
  (1 shorter events, 0.0 us)
Async XLA Ops:
  7.2 166.9 %all-gather.7.cloned.1.call-start = ((), (), s32[]{:S(2)}) async-start(), calls=%async_computation.1 | async-start | bytes 16908288 | tf_op jit(solution)/shard_map/all_gather | solution.py:258
  7.9 322.3 %all-gather.5.cloned.1.call-start = ((), (), s32[]{:S(2)}) async-start(), calls=%async_computation | async-start | bytes 16908288 | tf_op jit(solution)/shard_map/all_gather | solution.py:257
Sparse Core Ops, SparseCore 0:
  11.1 162.9 all-gather.6
  177.8 152.3 all-gather.4

commit v2 on v1

--- a/solution.py
+++ b/solution.py
@@ -12,6 +12,9 @@
 HIGH = lax.Precision.HIGH
 HIGHEST = lax.Precision.HIGHEST
 MESH = pl.DeviceIdType.MESH
+EIGHT = 8
+PIECES = 1
+UNROLL = 8
 GROUP = 8
 
 
@@ -156,85 +159,88 @@
     last = pl.num_programs(0) - 1
     me = lax.axis_index("tm")
 
-    def transform(slab, dst):
-        src = slab.reshape(shards * rows, block)
-
-        @pl.loop(0, rows // 2)
-        def _(pair):
-            p = pair * 2
-            x = jnp.concatenate([
-                src[pl.ds(p, shards, stride=rows), :],
-                src[pl.ds(p + 1, shards, stride=rows), :]], axis=0)
-            high, low = split(x)
+    def transform(src, dst):
+        planes = dst.reshape(2 * block, rows, shards)
+
+        @pl.loop(0, rows // EIGHT)
+        def _(part):
+            at = pl.multiple_of(part * EIGHT, EIGHT)
+            x = jnp.swapaxes(src[:, pl.ds(at, EIGHT), :], 0, 1)
+            high, low = split(x.reshape(EIGHT * shards, block))
             both = jnp.concatenate([high, low], axis=1)
-            out = outer(fhh_ref[...], both) + outer(fl_ref[...], high)
-            dst[pl.ds(p, 2 * block, stride=rows), :] = out[:, :shards]
-            dst[pl.ds(p + 1, 2 * block, stride=rows), :] = out[:, shards:]
+            for piece in range(PIECES):
+                span = slice(piece * 2 * block // PIECES, (piece + 1) * 2 * block // PIECES)
+                out = outer(fhh_ref[span], both) + outer(fl_ref[span], high)
+                out = jnp.stack([out[:, k * shards:(k + 1) * shards] for k in range(EIGHT)])
+                planes[span, pl.ds(at, EIGHT), :] = jnp.swapaxes(out, 0, 1)
 
     transform(x_ref, hx)
     transform(s_ref, hs)
 
-    def product(f):
+    def product(f, parity):
         at = pl.multiple_of(f * 2 * rows, 2 * rows)
         h = hx[pl.ds(at, 2 * rows), :]
-        t_re = hs[pl.ds(at, rows), :]
-        t_im = hs[pl.ds(at + rows, rows), :]
-        sign = (1 - 2 * lax.rem(f, 2)).astype(jnp.float32)
-        here = pltpu.roll(jnp.concatenate([t_re, t_im], axis=0), me, 1)
-        past = pltpu.roll(jnp.concatenate([-t_im, t_re], axis=0), me + 1, 1)
-        t = here + sign * past
+        t = hs[pl.ds(at, 2 * rows), :]
+        past = pltpu.roll(t, me + 1, 1)
+        past = jnp.concatenate([-past[rows:], past[:rows]], axis=0)
+        here = pltpu.roll(t, me, 1)
+        t = here + past if parity == 0 else here - past
         hh, hl = split(h)
         th, tl = split(t)
         return outer(jnp.concatenate([hh, hl], axis=1), jnp.concatenate([th, th], axis=1)) + outer(hh, tl)
 
-    @pl.when(step == 0)
-    def _():
-        @pl.loop(0, block)
-        def _(f):
-            mix[pl.ds(f, 2 * rows, stride=block), :] = product(f)
-
-    @pl.when(step != 0)
-    def _():
-        @pl.loop(0, block)
-        def _(f):
-            mix[pl.ds(f, 2 * rows, stride=block), :] += product(f)
+    def products(first):
+        @pl.loop(0, block // UNROLL)
+        def _(turn):
+            for k in range(UNROLL):
+                f = turn * UNROLL + k
+                span = pl.ds(pl.multiple_of(f * 2 * rows, 2 * rows), 2 * rows)
+                value = product(f, k % 2)
+                mix[span, :] = value if first else mix[span, :] + value
+
+    pl.when(step == 0)(lambda: products(True))
+    pl.when(step != 0)(lambda: products(False))
 
     @pl.when(step == last)
     def _():
         gram_ref[...] = jnp.zeros_like(gram_ref)
-
-        @pl.loop(0, rows // 2)
-        def _(pair):
-            def parts(p):
-                zero = mix[pl.ds(pl.multiple_of(p * block, block), block), :]
-                one = mix[pl.ds(pl.multiple_of((rows + p) * block, block), block), :]
-                return zero + pltpu.roll(one, rows, 1), one - pltpu.roll(zero, rows, 1)
-
-            re0, im0 = parts(pair * 2)
-            re1, im1 = parts(pair * 2 + 1)
-            lane = lax.broadcasted_iota(jnp.int32, re0.shape, 1)
-            re = jnp.where(lane < rows, re0, pltpu.roll(re1, rows, 1))
-            im = jnp.where(lane < rows, im0, pltpu.roll(im1, rows, 1))
-            high, low = split(jnp.concatenate([re, im], axis=0))
-            out = inner(bh_ref[...], high) + inner(bh_ref[...], low) + inner(bl_ref[...], high)
-            sig = out.T
-            sig_ref[pl.ds(pl.multiple_of(pair * 2 * rows, 2 * rows), 2 * rows), :] = sig
-            gram_ref[...] += lax.dot_general(
-                sig, sig, (((1,), (1,)), ((), ())), precision=HIGHEST,
-                preferred_element_type=jnp.float32)
-
-
-def image(all_m, all_s, block, shards, rows, inputs):
+        planes = mix.reshape(block, 2 * rows, 2 * rows)
+        lane = lax.broadcasted_iota(jnp.int32, (block, 2 * rows), 1)
+
+        @pl.loop(0, rows // EIGHT)
+        def _(part):
+            at = pl.multiple_of(part * EIGHT, EIGHT)
+            zeros = jnp.swapaxes(planes[:, pl.ds(at, EIGHT), :], 0, 1)
+            ones = jnp.swapaxes(planes[:, pl.ds(rows + at, EIGHT), :], 0, 1)
+
+            def parts(k):
+                return zeros[k] + pltpu.roll(ones[k], rows, 1), ones[k] - pltpu.roll(zeros[k], rows, 1)
+
+            for k in range(0, EIGHT, 2):
+                re0, im0 = parts(k)
+                re1, im1 = parts(k + 1)
+                re = jnp.where(lane < rows, re0, pltpu.roll(re1, rows, 1))
+                im = jnp.where(lane < rows, im0, pltpu.roll(im1, rows, 1))
+                high, low = split(jnp.concatenate([re, im], axis=0))
+                out = inner(bh_ref[...], high) + inner(bh_ref[...], low) + inner(bl_ref[...], high)
+                sig = out.T
+                sig_ref[pl.ds(pl.multiple_of((at + k) * rows, 2 * rows), 2 * rows), :] = sig
+                gram_ref[...] += lax.dot_general(
+                    sig, sig, (((1,), (1,)), ((), ())), precision=HIGHEST,
+                    preferred_element_type=jnp.float32)
+
+
+def image(gathered, block, shards, rows, inputs):
     tables = waves(block)
     assert block == shards == 2 * rows
     whole = lambda x: pl.BlockSpec(x.shape, lambda m: (0, 0), pipeline_mode=pl.Buffered(1))
-    slab = pl.BlockSpec((shards, None, rows, block), lambda m: (0, m, 0, 0))
+    slab = lambda first: pl.BlockSpec((shards, None, rows, block), lambda m: (0, first + m, 0, 0))
     return pl.pallas_call(
         functools.partial(spectrum_kernel, block, shards, rows),
         grid=(inputs,),
         out_shape=(jax.ShapeDtypeStruct((rows * rows, block), jnp.float32),
                    jax.ShapeDtypeStruct((2 * rows, 2 * rows), jnp.float32)),
-        in_specs=[slab, slab] + [whole(x) for x in tables],
+        in_specs=[slab(0), slab(inputs)] + [whole(x) for x in tables],
         out_specs=(pl.BlockSpec((rows * rows, block), lambda m: (0, 0)),
                    pl.BlockSpec((2 * rows, 2 * rows), lambda m: (0, 0))),
         scratch_shapes=[pltpu.VMEM((2 * block * rows, shards), jnp.float32),
@@ -242,7 +248,7 @@
                         pltpu.VMEM((2 * rows * block, 2 * rows), jnp.float32)],
         compiler_params=pltpu.CompilerParams(
             dimension_semantics=("arbitrary",), vmem_limit_bytes=60 * 2**20),
-    )(all_m, all_s, *tables)
+    )(gathered, gathered, *tables)
 
 
 def body(markov, sketch):
@@ -254,9 +260,8 @@
 
     own_m = markov.transpose(2, 1, 0)
     own_s = sketch.transpose(1, 2, 0)
-    all_m = lax.all_gather(own_m, "tm", axis=0, tiled=False)
-    all_s = lax.all_gather(own_s, "tm", axis=0, tiled=False)
-    sig, gram_two = image(all_m, all_s, block, shards, channels, inputs)
+    gathered = lax.all_gather(jnp.concatenate([own_m, own_s]), "tm", axis=0, tiled=False)
+    sig, gram_two = image(gathered, block, shards, channels, inputs)
     signal = sig.reshape(channels, columns, block)
     gram_part = gram_two[:columns, :columns] + gram_two[columns:, columns:]
     gram = total_gram(gram_part, shards // GROUP, width)

time: 681 us -> 360 us (0.53)
  Pallas kernels: 324 us -> 120 us
  waiting for transfers between devices: 321 us -> 202 us
    pallas_call x1, Pallas kernels: 298 us -> 93.4 us  [image(): pl.pallas_call(functools.partial(spectrum_kernel, block, shards, rows), g...]
    all_gather x2 -> x1, waiting for transfers between devices: 321 us -> 202 us  [body(): lax.all_gather(jnp.concatenate([own_m, own_s]), 'tm', axis=0, tiled=False)]
  transfers between devices with their start and end apart: 2 -> 1, of which waited for: 2 -> 1; matrix products, arithmetic and copies ran while one was open for 0% -> 0% of each run, Pallas kernels for 0% -> 0%
where the time goes in v2:
time: 360 us; the launch traced here: 359 us
  waiting for transfers between devices  202 us (56%)
  Pallas kernels  120 us (33%)
  other arithmetic  16.7 us (5%)
  between operations  14.1 us (4%)
  matrix products  4.1 us (1%)
    all_gather x1, waiting for transfers between devices, body(): lax.all_gather(jnp.concatenate([own_m, own_s]), 'tm', axis=0, tiled=False)  202 us
    pallas_call x1, Pallas kernels, image(): pl.pallas_call(functools.partial(spectrum_kernel, block, shards, rows), g...  93.4 us
    pallas_call x1, Pallas kernels, total_gram(): pl.pallas_call(functools.partial(reduce_kernel, depth, width), out_shape=...  26.9 us
  transfers between devices with their start and end apart: 1, of which 1 were waited for; matrix products, arithmetic and copies ran while one was open for 0% of the time, Pallas kernels for 0%

profile of v2, /device:TPU:1, one launch (start us, length us, event | category | flops | bytes accessed | tf_op | source)
XLA Modules:
  0.0 359.2 jit_solution(7326686403085983501)
XLA Ops:
  7.2 0.0 all-gather.3.cloned.1.call-start
  7.2 0.9 copy.19
  8.1 1.6 pad_maximum_fusion
  9.8 0.0 all-gather.3.cloned.1.call-update
  9.8 202.3 %all-gather.3.cloned.1.call-done = f32[1024,64,128]{2,1,0:T(8,128)} async-done(((f32[8,64,128]{2,1,0:T(8,128)}), f32[1024,64,128]{2,1,0:T(8,128)}) %all-gather.3.cloned.1.call-update) | async-done | bytes 33554448 | tf_op jit(solution)/shard_map/all_gather | solution.py:263
  212.0 93.4 %shard_map.77 = (f32[4096,128]{1,0:T(8,128)}, f32[128,128]{1,0:T(8,128)}) custom-call(f32[128,8,64,128]{3,2,1,0:T(8,128)} %bitcast.29, f32[128,8,64,128]{3,2,1,0:T(8,128)} %bitcast.30, bf16[256,256]{1,0:T(8,128)(2,1)} %constant.54.clone.fhh_ref, bf16[256,128]{1,0:T(8,128)(2,1)} %constant.55.clone.fl_ref, bf16[128,256]{1,0:T(8,128)(2,1)} %constant.56.clone.bh_ref, ...), custom_call_target="tpu_custom_call" | custom-call | tf_op jit(solution)/shard_map/pallas_call | solution.py:238
  305.5 1.5 add_bitcast_fusion.gram_ref
  306.9 26.9 %shard_map.78 = f32[8,8,64]{2,1,0:T(8,128)} custom-call(f32[8,8,64]{2,1,0:T(8,128)} %add_bitcast_fusion.gram_ref), custom_call_target="tpu_custom_call" | custom-call | tf_op jit(solution)/shard_map/pallas_call | solution.py:103
  333.8 0.8 multiply_bitcast_fusion
  334.6 0.1 copy.16
  334.7 0.8 fusion.1
  335.4 5.8 %cholesky.17 = f32[64,64]{1,0:T(8,128)S(1)} custom-call(f32[64,64]{1,0:T(8,128)S(1)} %fusion.1), custom_call_target="Cholesky" | custom-call | tf_op jit(solution)/shard_map/jit(cholesky)/cholesky | solution.py:268
  341.3 0.6 compare_reduce_fusion
  342.0 0.7 fusion.2
  342.6 0.7 copy.17
  343.3 4.9 %custom-call.7 = f32[1,64,64]{1,2,0:T(8,128)S(1)} custom-call(f32[1,64,64]{2,1,0:T(8,128)S(1)} %get-tuple-element.13), custom_call_target="InvertDiagBlocksLowerTriangular" | custom-call | tf_op jit(solution)/shard_map/jit(_solve_triangular)/triangular_solve | solution.py:270
  348.2 0.2 convolution_bitcast_fusion.1
  348.5 3.9 %convolution_bitcast_fusion = f32[128,64,64]{0,2,1:T(8,128)} fusion(f32[64,64,1]{1,0,2:T(8,128)S(1)} %convolution_bitcast_fusion.1, f32[64,64,128]{2,1,0:T(8,128)} %bitcast.31), kind=kOutput, calls=%fused_computation | convolution fusion | flops 201326592 | bytes 4210688 | tf_op jit(solution)/shard_map/prb,rs->bps/dot_general | solution.py:271
  (1 shorter events, 0.0 us)
Async XLA Ops:
  7.2 204.9 %all-gather.3.cloned.1.call-start = ((), (), s32[]{:S(2)}) async-start(), calls=%async_computation | async-start | bytes 33816576 | tf_op jit(solution)/shard_map/all_gather | solution.py:263
Sparse Core Ops, SparseCore 0:
  11.7 200.3 all-gather.2

commit v3 on v2

--- a/solution.py
+++ b/solution.py
@@ -15,6 +15,8 @@
 EIGHT = 8
 PIECES = 1
 UNROLL = 8
+SPLIT = 5
+RING = 4
 GROUP = 8
 
 
@@ -123,6 +125,124 @@
     )(part.reshape((GROUP,) + tile)).reshape(64, 64)
 
 
+def gather_kernel(depth, x_ref, out_ref, own_sem, send_sems, recv_sems):
+    tm = lax.axis_index("tm")
+    ch = lax.axis_index("chan")
+    z = tm // GROUP
+    y = (tm - z * GROUP) // 2
+    core = tm - z * GROUP - y * 2
+    half = x_ref.shape[1] // 2
+    lower, upper = pl.ds(0, half), pl.ds(half, half)
+    head, tail = pl.ds(0, SPLIT), pl.ds(SPLIT, x_ref.shape[0] - SPLIT)
+    turn = lambda k: lax.rem(z + k + depth, depth)
+    side = lambda k: lax.rem(y + k + RING, RING)
+    device = lambda zi, yi, ci: ((zi * RING + yi) * 2 + ci, ch)
+    up, down = device(turn(1), y, core), device(turn(-1), y, core)
+    right, left = device(z, side(1), core), device(z, side(-1), core)
+    other = device(z, y, 1 - core)
+
+    barrier = pltpu.get_barrier_semaphore()
+    for peer in (up, down, right, left, other):
+        pl.semaphore_signal(barrier, inc=1, device_id=peer, device_id_type=MESH)
+    pl.semaphore_wait(barrier, 5)
+
+    copies = []
+
+    def send(part, to, source=None):
+        slot = len(copies)
+        copy = pltpu.make_async_remote_copy(
+            src_ref=part if source is None else source, dst_ref=part,
+            send_sem=send_sems.at[slot], recv_sem=recv_sems.at[slot],
+            device_id=to, device_id_type=MESH)
+        copy.start()
+        copies.append(copy)
+        return copy
+
+    def received(*some):
+        for copy in some:
+            copy.wait_recv()
+
+    def along_y(zi, source=None):
+        part = out_ref.at[zi, y, core, head]
+        return zi, send(part, right, source), send(part, left, source)
+
+    def across_y(zi, one, two):
+        received(one, two)
+        return (zi, send(out_ref.at[zi, side(-1), core, head, lower], right),
+                send(out_ref.at[zi, side(1), core, head, upper], left))
+
+    last = []
+
+    def to_core(zi, rows):
+        last.append(send(out_ref.at[zi, :, core, rows], other))
+
+    own = pltpu.make_async_copy(x_ref, out_ref.at[z, y, core], own_sem)
+    own.start()
+    first = x_ref.at[head]
+    second = x_ref.at[tail]
+    row = out_ref.at[z, y, core, tail]
+    b_right, b_left = send(row, right, second), send(row, left, second)
+    a_up = send(out_ref.at[z, y, core, head], up, first)
+    a_down = send(out_ref.at[z, y, core, head], down, first)
+    received(b_right, b_left)
+    b_right = send(out_ref.at[z, side(-1), core, tail, lower], right)
+    b_left = send(out_ref.at[z, side(1), core, tail, upper], left)
+    direct = [along_y(z, first)]
+    own.wait()
+    received(b_right, b_left)
+    b_up = send(out_ref.at[z, :, core, tail], up)
+    b_down = send(out_ref.at[z, :, core, tail], down)
+    to_core(z, tail)
+    crossing = []
+    middle = depth // 2
+    for step in range(1, middle + 1):
+        received(a_up, a_down)
+        zu, zd = turn(-step), turn(step)
+        if step < middle - 1:
+            a_up = send(out_ref.at[zu, y, core, head], up)
+            a_down = send(out_ref.at[zd, y, core, head], down)
+        elif step == middle - 1:
+            a_up = send(out_ref.at[zu, y, core, head, lower], up)
+            a_down = send(out_ref.at[zd, y, core, head, upper], down)
+        for block in crossing:
+            received(*block[1:])
+            to_core(block[0], head)
+        crossing = [across_y(*block) for block in direct]
+        direct = [along_y(zu)] + ([along_y(zd)] if step < middle else [])
+        received(b_up, b_down)
+        if step < middle - 1:
+            b_up = send(out_ref.at[zu, :, core, tail], up)
+            b_down = send(out_ref.at[zd, :, core, tail], down)
+        elif step == middle - 1:
+            b_up = send(out_ref.at[zu, :, core, tail, lower], up)
+            b_down = send(out_ref.at[zd, :, core, tail, upper], down)
+        to_core(zu, tail)
+        if step < middle:
+            to_core(zd, tail)
+    final = [across_y(*block) for block in direct]
+    for block in crossing + final:
+        received(*block[1:])
+        to_core(block[0], head)
+    received(*last)
+    for copy in copies:
+        copy.wait_send()
+
+
+def gather(own, shards):
+    depth = shards // GROUP
+    count = 15 * depth
+    return pl.pallas_call(
+        functools.partial(gather_kernel, depth),
+        out_shape=jax.ShapeDtypeStruct((depth, RING, 2) + own.shape, jnp.float32),
+        in_specs=[pl.BlockSpec(memory_space=pltpu.VMEM)],
+        out_specs=pl.BlockSpec(memory_space=pl.ANY),
+        scratch_shapes=[pltpu.SemaphoreType.DMA,
+                        pltpu.SemaphoreType.DMA((count,)),
+                        pltpu.SemaphoreType.DMA((count,))],
+        compiler_params=pltpu.CompilerParams(collective_id=2, has_side_effects=True),
+    )(own).reshape((shards,) + own.shape)
+
+
 def split(x):
     high = x.astype(jnp.bfloat16)
     return high, (x - high.astype(jnp.float32)).astype(jnp.bfloat16)
@@ -260,7 +380,7 @@
 
     own_m = markov.transpose(2, 1, 0)
     own_s = sketch.transpose(1, 2, 0)
-    gathered = lax.all_gather(jnp.concatenate([own_m, own_s]), "tm", axis=0, tiled=False)
+    gathered = gather(jnp.concatenate([own_m, own_s]), shards)
     sig, gram_two = image(gathered, block, shards, channels, inputs)
     signal = sig.reshape(channels, columns, block)
     gram_part = gram_two[:columns, :columns] + gram_two[columns:, columns:]

time: 360 us -> 270 us (0.75)
  waiting for transfers between devices: 202 us -> 0 us
  Pallas kernels: 120 us -> 246 us
  between operations: 14.1 us -> 0.67 us
    all_gather x1 -> x0, waiting for transfers between devices: 202 us -> none  [body(): lax.all_gather(jnp.concatenate([own_m, own_s]), 'tm', axis=0, tiled=False)]
    pallas_call x0 -> x1, Pallas kernels: none -> 127 us  [gather(): pl.pallas_call(functools.partial(gather_kernel, depth), out_shape=jax.Sha...]
  transfers between devices with their start and end apart: 1 -> 0, of which waited for: 1 -> 0; matrix products, arithmetic and copies ran while one was open for 0% -> 0% of each run, Pallas kernels for 0% -> 0%
where the time goes in v3:
time: 270 us; the launch traced here: 269 us
  Pallas kernels  246 us (91%)
  other arithmetic  16.7 us (6%)
  matrix products  4.1 us (2%)
    pallas_call x1, Pallas kernels, gather(): pl.pallas_call(functools.partial(gather_kernel, depth), out_shape=jax.Sha...  127 us
    pallas_call x1, Pallas kernels, image(): pl.pallas_call(functools.partial(spectrum_kernel, block, shards, rows), g...  93.5 us
    pallas_call x1, Pallas kernels, total_gram(): pl.pallas_call(functools.partial(reduce_kernel, depth, width), out_shape=...  25.9 us
    another operation x3, other arithmetic, body(): lower = jnp.linalg.cholesky(gram / row_total)  6.52 us

profile of v3, /device:TPU:1, one launch (start us, length us, event | category | flops | bytes accessed | tf_op | source)
XLA Modules:
  0.0 269.2 jit_solution(4739419635062508656)
XLA Ops:
  0.6 0.9 copy.16
  1.5 1.6 pad_maximum_fusion.x_ref
  3.2 126.7 %shard_map.77 = f32[16,4,2,8,64,128]{5,4,3,2,1,0:T(8,128)} custom-call(f32[8,64,128]{2,1,0:T(8,128)} %pad_maximum_fusion.x_ref), custom_call_target="tpu_custom_call" | custom-call | tf_op jit(solution)/shard_map/pallas_call | solution.py:234
  129.9 93.5 %shard_map.78 = (f32[4096,128]{1,0:T(8,128)}, f32[128,128]{1,0:T(8,128)}) custom-call(f32[128,8,64,128]{3,2,1,0:T(8,128)} %bitcast.29, f32[128,8,64,128]{3,2,1,0:T(8,128)} %bitcast.30, bf16[256,256]{1,0:T(8,128)(2,1)} %constant.54.clone.fhh_ref, bf16[256,128]{1,0:T(8,128)(2,1)} %constant.55.clone.fl_ref, bf16[128,256]{1,0:T(8,128)(2,1)} %constant.56.clone.bh_ref, ...), custom_call_target="tpu_custom_call" | custom-call | tf_op jit(solution)/shard_map/pallas_call | solution.py:358
  223.3 1.5 add_bitcast_fusion.gram_ref
  224.8 25.9 %shard_map.79 = f32[8,8,64]{2,1,0:T(8,128)} custom-call(f32[8,8,64]{2,1,0:T(8,128)} %add_bitcast_fusion.gram_ref), custom_call_target="tpu_custom_call" | custom-call | tf_op jit(solution)/shard_map/pallas_call | solution.py:105
  250.7 0.8 multiply_bitcast_fusion
  251.5 0.1 copy.13
  251.6 0.8 fusion.1
  252.4 5.8 %cholesky.17 = f32[64,64]{1,0:T(8,128)S(1)} custom-call(f32[64,64]{1,0:T(8,128)S(1)} %fusion.1), custom_call_target="Cholesky" | custom-call | tf_op jit(solution)/shard_map/jit(cholesky)/cholesky | solution.py:388
  258.2 0.6 compare_reduce_fusion
  258.9 0.7 fusion.2
  259.5 0.7 copy.14
  260.2 4.9 %custom-call.7 = f32[1,64,64]{1,2,0:T(8,128)S(1)} custom-call(f32[1,64,64]{2,1,0:T(8,128)S(1)} %get-tuple-element.11), custom_call_target="InvertDiagBlocksLowerTriangular" | custom-call | tf_op jit(solution)/shard_map/jit(_solve_triangular)/triangular_solve | solution.py:390
  265.1 0.2 convolution_bitcast_fusion.1
  265.4 3.9 %convolution_bitcast_fusion = f32[128,64,64]{0,2,1:T(8,128)} fusion(f32[64,64,1]{1,0,2:T(8,128)S(1)} %convolution_bitcast_fusion.1, f32[64,64,128]{2,1,0:T(8,128)} %bitcast.31), kind=kOutput, calls=%fused_computation | convolution fusion | flops 201326592 | bytes 4210688 | tf_op jit(solution)/shard_map/prb,rs->bps/dot_general | solution.py:391
  (1 shorter events, 0.0 us)
